TPU v7x, 256 devices: a whole 4x4x8 slice. The times are simulated.
256 devices in a mesh: row: 8 (over y, core), col: 8 (over x, z_hi), rep: 4 (over z_lo).
Axes of the slice: x: 4, y: 4, z: 8 (z_hi: 2, z_lo: 4; z = z_hi * 4 + z_lo), core: 2. Of those that a mesh axis runs over, the one named last changes fastest.
Arguments:
- features: float32 [256, 32768], P('rep', ('col', 'row')), may hold values from -6 to 6
- weight: float32 [256, 256], replicated, may hold values from -0.375 to 0.375
- cotangent: float32 [256, 32768], P('rep', ('row', 'col')), may hold values from -6 to 6
- tile_values: float32 [10240, 128, 128], P(('row', 'col')), may hold values from -0.078125 to 0.078125
- tile_row: int32 [10240], P(('row', 'col')), may hold values from 0 to 31
- tile_col: int32 [10240], P(('row', 'col')), may hold values from 0 to 31
- tile_kind: int32 [10240], P(('row', 'col')), may hold values from 0 to 159
- tile_count: int32 [64], P(('row', 'col')), may hold values from 40 to 160, as said below
Outputs:
- output: float32 [256, 32768], P('rep', ('row', 'col'))
- input_grad: float32 [256, 32768], P('rep', ('col', 'row'))
- weight_grad: float32 [256, 256], P('rep')
Inputs may be any that keep to these rules, and one draw needn't show every extreme that they name: `tile_count`: a block's slots at or after its count are not part of the adjacency; some block uses all 160 slots. `tile_row`: slots may repeat a tile position; their tiles add. `tile_kind`: an index into the 160 stored tiles of the same block.
All inputs are finite; a program needn't handle non-finite values.
Results may differ from a plain program's by a relative error of at most 0.0001.
Values sent between devices are 32-bit elements; how exact they have to be, the bound alone decides.
No kernel may reach another device: no remote copies, remote signals or barrier semaphores. Data moves between devices by JAX's collectives and lax.ppermute only.
A program may use at most 128 MiB of HBM per device.

v0:
```python
import jax
import jax.numpy as jnp
from jax import lax
from jax.sharding import PartitionSpec as P


def tile_terms(source, values, from_tile, to_tile, tile_kinds, live_weight, dest_tiles, transposed):
    feat_width = source.shape[0]
    tile_edge = values.shape[1]
    tiled = source.reshape(feat_width, source.shape[1] // tile_edge, tile_edge)
    picked = jnp.take(tiled, from_tile, axis=1)
    chosen = jnp.take(values, tile_kinds, axis=0)
    if transposed:
        products = jnp.einsum("fga,gab->fgb", picked, chosen, precision=lax.Precision.HIGHEST)
    else:
        products = jnp.einsum("fgb,gab->fga", picked, chosen, precision=lax.Precision.HIGHEST)
    onehot = (to_tile[:, None] == jnp.arange(dest_tiles, dtype=jnp.int32)[None, :]).astype(
        jnp.float32
    )
    onehot = onehot * live_weight[:, None]
    spread = jnp.einsum("fgt,gd->fdt", products, onehot, precision=lax.Precision.HIGHEST)
    return spread.reshape(feat_width, dest_tiles * tile_edge)


def aggregate(source, values, from_tile, to_tile, tile_kinds, live_count, dest_tiles, transposed):
    slot_total = tile_kinds.shape[0]
    live_weight = (jnp.arange(slot_total, dtype=jnp.int32) < live_count).astype(jnp.float32)
    return tile_terms(
        source, values, from_tile, to_tile, tile_kinds, live_weight, dest_tiles, transposed
    )


def local(features, weight, cotangent, tile_values, tile_row, tile_col, tile_kind, tile_count):
    n_rowdev = lax.axis_size("row")
    n_coldev = lax.axis_size("col")
    n_repdev = lax.axis_size("rep")
    quarter = weight.shape[0] // n_repdev
    rep_index = lax.axis_index("rep")
    own_rows = lax.dynamic_slice_in_dim(weight, rep_index * quarter, quarter, 0)
    own_cols = lax.dynamic_slice_in_dim(weight, rep_index * quarter, quarter, 1)
    stretch_len = features.shape[1]
    tile_edge = tile_values.shape[1]
    live_count = tile_count[0]
    row_tiles = n_coldev * stretch_len // tile_edge
    col_tiles = n_rowdev * stretch_len // tile_edge
    mixed = lax.psum_scatter(
        lax.dot_general(
            own_rows,
            features,
            (((0,), (0,)), ((), ())),
            precision=lax.Precision.HIGHEST,
            preferred_element_type=jnp.float32,
        ),
        "rep",
        scatter_dimension=0,
        tiled=True,
    )
    column_block = lax.all_gather(mixed, "row", axis=1, tiled=True)
    partial_value = aggregate(
        column_block, tile_values, tile_col, tile_row, tile_kind, live_count, row_tiles, False
    )
    summed = lax.psum_scatter(partial_value, "col", scatter_dimension=1, tiled=True)
    output, pullback = jax.vjp(lambda v: jax.nn.gelu(v, approximate=True), summed)
    (grad_pre,) = pullback(cotangent)
    row_block = lax.all_gather(grad_pre, "col", axis=1, tiled=True)
    partial_back = aggregate(
        row_block, tile_values, tile_row, tile_col, tile_kind, live_count, col_tiles, True
    )
    grad_mixed = lax.psum_scatter(partial_back, "row", scatter_dimension=1, tiled=True)
    input_grad = lax.psum_scatter(
        jnp.dot(
            own_cols,
            grad_mixed,
            preferred_element_type=jnp.float32,
            precision=lax.Precision.HIGHEST,
        ),
        "rep",
        scatter_dimension=0,
        tiled=True,
    )
    weight_part = lax.dot_general(
        features,
        lax.all_gather(grad_mixed, "rep", axis=0, tiled=True),
        (((1,), (1,)), ((), ())),
        precision=lax.Precision.HIGHEST,
        preferred_element_type=jnp.float32,
    )
    node_total = stretch_len * n_rowdev * n_coldev
    weight_grad = lax.psum(weight_part * float(node_total) ** (-0.5), ("row", "col"))
    return (output, input_grad, weight_grad)


def solution(mesh):
    return jax.shard_map(
        local,
        mesh=mesh,
        in_specs=(
            P("rep", ("col", "row")),
            P(),
            P("rep", ("row", "col")),
            P(("row", "col"), None, None),
            P(("row", "col")),
            P(("row", "col")),
            P(("row", "col")),
            P(("row", "col")),
        ),
        out_specs=(P("rep", ("row", "col")), P("rep", ("col", "row")), P("rep", None)),
        check_vma=False,
    )
```

profile of v0, /device:TPU:2, one launch (start us, length us, event | category | flops | bytes accessed | tf_op | source)
XLA Modules:
  0.0 1082.4 jit_solution(2901445615518222513)
XLA Ops:
  7.2 0.9 copy-done
  8.1 2.3 fusion.39
  10.5 0.0 all-gather.3.cloned.1.call-start
  10.5 30.2 %reduce-scatter.5.cloned.1.call-done = f32[64,512]{1,0:T(8,128)} async-done(((f32[256,512]{1,0:T(8,128)}), f32[64,512]{1,0:T(8,128)}) %reduce-scatter.5.cloned.1.call-update) | async-done | bytes 131088 | tf_op jit(solution)/shard_map/reduce_scatter | solution.py:46
  40.7 0.0 reduce-scatter.7.cloned.1.call-start
  41.4 0.7 compare_select_fusion.2
  42.1 14.2 %gather_fusion = f32[160,128,128]{2,1,0:T(8,128)} fusion(f32[160,128,128]{2,1,0:T(8,128)} %param.15, s32[1024]{0:T(1024)S(1)} %pad_clamp_fusion.2), kind=kCustom, calls=%fused_computation.clone | custom fusion | bytes 20972160 | tf_op jit(solution)/shard_map/jit(_take)/gather | solution.py:12
  56.3 10.5 all-gather.3.cloned.1.call-done
  66.8 1.3 copy_bitcast_fusion.3
  68.2 3.3 gather_fusion.1
  71.5 24.3 %fusion.20 = f32[64,160,128]{2,0,1:T(8,128)S(1)} fusion(f32[160,64,128]{2,1,0:T(8,128)} %gather_fusion.1, pred[160]{0:T(512)(128)(4,1)S(1)} %get-tuple-element.7, f32[160,128,128]{2,1,0:T(8,128)} %gather_fusion, pred[160]{0:T(512)(128)(4,1)S(1)} %get-tuple-element.8), kind=kOutput, calls=%fused_computation.23 | convolution fusion | flops 2017198080 | bytes 20971840 | tf_op jit(solution)/shard_map/fgb,gab->fga/dot_general | solution.py:16
  95.8 5.6 fusion.8
  101.5 1.6 copy.29
  103.1 0.0 all-gather.5.cloned.1.call-start
  103.1 87.2 %reduce-scatter.7.cloned.1.call-done = f32[64,512]{1,0:T(8,128)} async-done(((f32[64,4096]{1,0:T(8,128)}), f32[64,512]{1,0:T(8,128)}) %reduce-scatter.7.cloned.1.call-update) | async-done | bytes 131088 | tf_op jit(solution)/shard_map/reduce_scatter | solution.py:62
  190.4 1.7 fusion.36
  192.1 0.0 reduce-scatter.9.cloned.1.call-start
  192.2 59.1 %all-gather.5.cloned.1.call-done = f32[64,4096]{1,0:T(8,128)} async-done(((f32[64,512]{1,0:T(8,128)}), f32[64,4096]{1,0:T(8,128)}) %all-gather.5.cloned.1.call-update) | async-done | bytes 1048592 | tf_op jit(solution)/shard_map/all_gather | solution.py:65
  251.3 1.3 copy_bitcast_fusion.2
  252.7 3.3 gather_fusion.2
  255.9 13.9 %fusion.25 = f32[64,160,128]{2,0,1:T(8,128)S(1)} fusion(f32[160,64,128]{2,1,0:T(8,128)} %gather_fusion.2, pred[160]{0:T(512)(128)(4,1)S(1)} %compare_and_fusion, f32[160,128,128]{2,1,0:T(8,128)} %gather_fusion, pred[160]{0:T(512)(128)(4,1)S(1)} %get-tuple-element.8), kind=kOutput, calls=%fused_computation.24 | convolution fusion | flops 2017198080 | bytes 20971840 | tf_op jit(solution)/shard_map/fga,gab->fgb/dot_general | solution.py:14
  269.8 5.6 fusion.6
  275.5 1.6 copy.28
  277.1 0.0 all-reduce.2.cloned.1.call-start
  277.1 30.8 %reduce-scatter.9.cloned.1.call-done = f32[64,512]{1,0:T(8,128)} async-done(((f32[64,4096]{1,0:T(8,128)}), f32[64,512]{1,0:T(8,128)}) %reduce-scatter.9.cloned.1.call-update) | async-done | bytes 131088 | tf_op jit(solution)/shard_map/reduce_scatter | solution.py:69
  307.9 16.4 %all_gather.11 = f32[256,512]{1,0:T(8,128)S(1)} all-gather(f32[64,512]{1,0:T(8,128)} %reduce-scatter.9.cloned.1.call-done), channel_id=1, replica_groups=mesh['row'=8,'col'=8,'rep'=4] {'rep'}, dimensions={0}, use_global_device_ids=true | all-gather | bytes 655360 | tf_op jit(solution)/shard_map/all_gather | solution.py:83
  324.4 1.2 fusion.30
  325.6 0.0 reduce-scatter.11.cloned.1.call-start
  325.7 2.3 fusion.37
  328.0 722.2 %all-reduce.2.cloned.1.call-done = f32[64,256]{1,0:T(8,128)} async-done(((f32[64,256]{1,0:T(8,128)}), f32[64,256]{1,0:T(8,128)}) %all-reduce.2.cloned.1.call-update) | async-done | bytes 65552 | tf_op jit(solution)/shard_map/psum | solution.py:89
  1050.2 23.9 %reduce-scatter.11.cloned.1.call-done = f32[64,512]{1,0:T(8,128)} async-done(((f32[256,512]{1,0:T(8,128)}), f32[64,512]{1,0:T(8,128)}) %reduce-scatter.11.cloned.1.call-update) | async-done | bytes 131088 | tf_op jit(solution)/shard_map/reduce_scatter | solution.py:70
  1074.1 1.5 copy.32
  (27 shorter events, 0.2 us)
Async XLA Ops:
  7.2 1.0 copy-start
  7.2 33.5 %reduce-scatter.5.cloned.1.call-start = ((), (), s32[]{:S(2)}) async-start(), calls=%async_computation.4 | async-start | bytes 655360 | tf_op jit(solution)/shard_map/reduce_scatter | solution.py:46
  10.5 56.4 %all-gather.3.cloned.1.call-start = ((), (), s32[]{:S(2)}) async-start(), calls=%async_computation.5 | async-start | bytes 1179648 | tf_op jit(solution)/shard_map/all_gather | solution.py:58
  40.7 149.7 %reduce-scatter.7.cloned.1.call-start = ((), (), s32[]{:S(2)}) async-start(), calls=%async_computation.6 | async-start | bytes 1179648 | tf_op jit(solution)/shard_map/reduce_scatter | solution.py:62
  42.1 14.2 %copy-start.3 = (s32[160]{0:T(256)S(1)}, s32[160]{0:T(256)}, u32[]{:S(2)}) copy-start(s32[160]{0:T(256)} %param.17) | copy-start | bytes 1924
  42.1 14.2 %copy-start.5 = (s32[160]{0:T(256)S(1)}, s32[160]{0:T(256)}, u32[]{:S(2)}) copy-start(s32[160]{0:T(256)} %param.18) | copy-start | bytes 1924
  71.5 24.3 %copy-start.4 = (s32[160]{0:T(256)S(1)}, s32[160]{0:T(256)}, u32[]{:S(2)}) copy-start(s32[160]{0:T(256)} %param.16) | copy-start | bytes 1924
  95.8 94.6 %copy-start.2 = (f32[64,512]{1,0:T(8,128)S(1)}, f32[64,512]{1,0:T(8,128)}, u32[]{:S(2)}) copy-start(f32[64,512]{1,0:T(8,128)} %param.14) | copy-start | bytes 393220
  103.1 148.2 %all-gather.5.cloned.1.call-start = ((), (), s32[]{:S(2)}) async-start(), calls=%async_computation.7 | async-start | bytes 1179648 | tf_op jit(solution)/shard_map/all_gather | solution.py:65
  192.1 115.8 %reduce-scatter.9.cloned.1.call-start = ((), (), s32[]{:S(2)}) async-start(), calls=%async_computation.8 | async-start | bytes 1179648 | tf_op jit(solution)/shard_map/reduce_scatter | solution.py:69
  269.8 54.5 %copy-start.1 = (f32[64,512]{1,0:T(8,128)S(1)}, f32[64,512]{1,0:T(8,128)}, u32[]{:S(2)}) copy-start(f32[64,512]{1,0:T(8,128)} %param.12) | copy-start | bytes 393220
  277.1 773.1 %all-reduce.2.cloned.1.call-start = ((), (), s32[]{:S(2)}) async-start(), calls=%async_computation.10 | async-start | bytes 131072 | tf_op jit(solution)/shard_map/psum | solution.py:89
  325.6 748.5 %reduce-scatter.11.cloned.1.call-start = ((), (), s32[]{:S(2)}) async-start(), calls=%async_computation.9 | async-start | bytes 655360 | tf_op jit(solution)/shard_map/reduce_scatter | solution.py:70
Sparse Core Ops, SparseCore 0:
  10.6 30.0 reduce-scatter.4
  42.5 24.2 all-gather.2
  103.2 87.1 reduce-scatter.6
  193.4 57.8 all-gather.4
  277.2 30.6 reduce-scatter.8
  325.7 724.4 all-reduce.1
  1053.3 20.7 reduce-scatter.10
where the time goes:
time: 1080 us
  waiting for transfers between devices  964 us (89%)
  matrix products  55.3 us (5%)
  local copies, waits for them, and re-layouts  29 us (3%)
  blocking collectives  16.4 us (2%)
  between operations  14.9 us (1%)
    psum x1, waiting for transfers between devices, local(): lax.psum(weight_part * float(node_total) ** (-0.5), ('row', 'col'))  722 us
    reduce_scatter x1, waiting for transfers between devices, local(): lax.psum_scatter(partial_value, 'col', scatter_dimension=1, tiled=True)  87.2 us
    all_gather x1, waiting for transfers between devices, local(): row_block = lax.all_gather(grad_pre, 'col', axis=1, tiled=True)  59.1 us
    reduce_scatter x1, waiting for transfers between devices, local(): lax.psum_scatter(partial_back, 'row', scatter_dimension=1, tiled=True)  30.8 us
    reduce_scatter x1, waiting for transfers between devices, local(): lax.psum_scatter(lax.dot_general(own_rows, features, (((0,), (0,)), ((),...  30.2 us
    dot_general x1, matrix products, tile_terms(): jnp.einsum('fgb,gab->fga', picked, chosen, precision=lax.Precision.HIGHEST)  24.3 us
    reduce_scatter x1, waiting for transfers between devices, local(): lax.psum_scatter(jnp.dot(own_cols, grad_mixed, preferred_element_type=jnp...  23.9 us
  transfers between devices with their start and end apart: 7, of which 7 were waited for; matrix products, arithmetic and copies ran while one was open for 2% of the time, Pallas kernels for 0%

commit v1 on v0

--- a/solution.py
+++ b/solution.py
@@ -86,7 +86,7 @@
         preferred_element_type=jnp.float32,
     )
     node_total = stretch_len * n_rowdev * n_coldev
-    weight_grad = lax.psum(weight_part * float(node_total) ** (-0.5), ("row", "col"))
+    weight_grad = lax.psum(lax.psum(weight_part * float(node_total) ** (-0.5), "row"), "col")
     return (output, input_grad, weight_grad)
 
 

time: 1080 us -> 530 us (0.49)
  waiting for transfers between devices: 964 us -> 411 us
    psum x1 -> x2, waiting for transfers between devices: 722 us -> 167 us  [the longest x1 104 us: local(): lax.psum(lax.psum(weight_part * float(node_total) ** (-0.5), 'row'), 'col')]
  transfers between devices with their start and end apart: 7 -> 8, of which waited for: 7 -> 8; matrix products, arithmetic and copies ran while one was open for 2% -> 3% of each run, Pallas kernels for 0% -> 0%
where the time goes in v1:
time: 530 us; the launch traced here: 529 us
  waiting for transfers between devices  411 us (78%)
  matrix products  55.3 us (10%)
  local copies, waits for them, and re-layouts  29 us (5%)
  blocking collectives  16.4 us (3%)
  between operations  14.9 us (3%)
    psum x1, waiting for transfers between devices, local(): lax.psum(lax.psum(weight_part * float(node_total) ** (-0.5), 'row'), 'col')  104 us
    reduce_scatter x1, waiting for transfers between devices, local(): lax.psum_scatter(partial_value, 'col', scatter_dimension=1, tiled=True)  87.2 us
    psum x1, waiting for transfers between devices, local(): lax.psum(weight_part * float(node_total) ** (-0.5), 'row')  62.8 us
    all_gather x1, waiting for transfers between devices, local(): row_block = lax.all_gather(grad_pre, 'col', axis=1, tiled=True)  59.1 us
    reduce_scatter x1, waiting for transfers between devices, local(): lax.psum_scatter(partial_back, 'row', scatter_dimension=1, tiled=True)  30.8 us
    reduce_scatter x1, waiting for transfers between devices, local(): lax.psum_scatter(lax.dot_general(own_rows, features, (((0,), (0,)), ((),...  30.2 us
    reduce_scatter x1, waiting for transfers between devices, local(): lax.psum_scatter(jnp.dot(own_cols, grad_mixed, preferred_element_type=jnp...  26.3 us
    dot_general x1, matrix products, tile_terms(): jnp.einsum('fgb,gab->fga', picked, chosen, precision=lax.Precision.HIGHEST)  24.3 us
  transfers between devices with their start and end apart: 8, of which 8 were waited for; matrix products, arithmetic and copies ran while one was open for 3% of the time, Pallas kernels for 0%

profile of v1, /device:TPU:2, one launch (start us, length us, event | category | flops | bytes accessed | tf_op | source)
XLA Modules:
  0.0 529.2 jit_solution(2774833966080528476)
XLA Ops:
  7.2 0.9 copy-done
  8.1 2.3 fusion.39
  10.5 0.0 all-gather.3.cloned.1.call-start
  10.5 30.2 %reduce-scatter.5.cloned.1.call-done = f32[64,512]{1,0:T(8,128)} async-done(((f32[256,512]{1,0:T(8,128)}), f32[64,512]{1,0:T(8,128)}) %reduce-scatter.5.cloned.1.call-update) | async-done | bytes 131088 | tf_op jit(solution)/shard_map/reduce_scatter | solution.py:46
  41.4 0.7 compare_select_fusion.2
  42.1 14.2 %gather_fusion = f32[160,128,128]{2,1,0:T(8,128)} fusion(f32[160,128,128]{2,1,0:T(8,128)} %param.15, s32[1024]{0:T(1024)S(1)} %pad_clamp_fusion.2), kind=kCustom, calls=%fused_computation.clone | custom fusion | bytes 20972160 | tf_op jit(solution)/shard_map/jit(_take)/gather | solution.py:12
  56.3 10.5 %all-gather.3.cloned.1.call-done = f32[64,4096]{1,0:T(8,128)} async-done(((f32[64,512]{1,0:T(8,128)}), f32[64,4096]{1,0:T(8,128)}) %all-gather.3.cloned.1.call-update) | async-done | bytes 1048592 | tf_op jit(solution)/shard_map/all_gather | solution.py:58
  66.8 1.3 copy_bitcast_fusion.3
  68.2 3.3 gather_fusion.1
  71.5 24.3 %fusion.20 = f32[64,160,128]{2,0,1:T(8,128)S(1)} fusion(f32[160,64,128]{2,1,0:T(8,128)} %gather_fusion.1, pred[160]{0:T(512)(128)(4,1)S(1)} %get-tuple-element.7, f32[160,128,128]{2,1,0:T(8,128)} %gather_fusion, pred[160]{0:T(512)(128)(4,1)S(1)} %get-tuple-element.8), kind=kOutput, calls=%fused_computation.23 | convolution fusion | flops 2017198080 | bytes 20971840 | tf_op jit(solution)/shard_map/fgb,gab->fga/dot_general | solution.py:16
  95.8 5.6 %fusion.8 = f32[32,64,128]{2,0,1:T(8,128)S(1)} fusion(f32[64,160,128]{2,0,1:T(8,128)S(1)} %fusion.20, f32[160]{0:T(256)S(1)} %compare_convert_fusion, s32[160]{0:T(256)S(1)} %copy-done.4), kind=kOutput, calls=%fused_computation.11 | convolution fusion | flops 503326720 | bytes 6292736 | tf_op jit(solution)/shard_map/fgt,gd->fdt/dot_general | solution.py:21
  101.5 1.6 copy.29
  103.1 0.0 all-gather.5.cloned.1.call-start
  103.1 87.2 %reduce-scatter.7.cloned.1.call-done = f32[64,512]{1,0:T(8,128)} async-done(((f32[64,4096]{1,0:T(8,128)}), f32[64,512]{1,0:T(8,128)}) %reduce-scatter.7.cloned.1.call-update) | async-done | bytes 131088 | tf_op jit(solution)/shard_map/reduce_scatter | solution.py:62
  190.4 1.7 fusion.36
  192.1 0.0 reduce-scatter.9.cloned.1.call-start
  192.2 59.1 %all-gather.5.cloned.1.call-done = f32[64,4096]{1,0:T(8,128)} async-done(((f32[64,512]{1,0:T(8,128)}), f32[64,4096]{1,0:T(8,128)}) %all-gather.5.cloned.1.call-update) | async-done | bytes 1048592 | tf_op jit(solution)/shard_map/all_gather | solution.py:65
  251.3 1.3 copy_bitcast_fusion.2
  252.7 3.3 gather_fusion.2
  255.9 13.9 %fusion.25 = f32[64,160,128]{2,0,1:T(8,128)S(1)} fusion(f32[160,64,128]{2,1,0:T(8,128)} %gather_fusion.2, pred[160]{0:T(512)(128)(4,1)S(1)} %compare_and_fusion, f32[160,128,128]{2,1,0:T(8,128)} %gather_fusion, pred[160]{0:T(512)(128)(4,1)S(1)} %get-tuple-element.8), kind=kOutput, calls=%fused_computation.24 | convolution fusion | flops 2017198080 | bytes 20971840 | tf_op jit(solution)/shard_map/fga,gab->fgb/dot_general | solution.py:14
  269.8 5.6 %fusion.6 = f32[32,64,128]{2,0,1:T(8,128)S(1)} fusion(f32[64,160,128]{2,0,1:T(8,128)S(1)} %fusion.25, s32[160]{0:T(256)S(1)} %copy-done.3, f32[160]{0:T(256)S(1)} %compare_convert_fusion), kind=kOutput, calls=%fused_computation.9 | convolution fusion | flops 503326720 | bytes 6292736 | tf_op jit(solution)/shard_map/fgt,gd->fdt/dot_general | solution.py:21
  275.5 1.6 copy.28
  277.1 0.0 all-reduce.3.cloned.1.call-start
  277.1 30.8 %reduce-scatter.9.cloned.1.call-done = f32[64,512]{1,0:T(8,128)} async-done(((f32[64,4096]{1,0:T(8,128)}), f32[64,512]{1,0:T(8,128)}) %reduce-scatter.9.cloned.1.call-update) | async-done | bytes 131088 | tf_op jit(solution)/shard_map/reduce_scatter | solution.py:69
  307.9 16.4 %all_gather.11 = f32[256,512]{1,0:T(8,128)S(1)} all-gather(f32[64,512]{1,0:T(8,128)} %reduce-scatter.9.cloned.1.call-done), channel_id=1, replica_groups=mesh['row'=8,'col'=8,'rep'=4] {'rep'}, dimensions={0}, use_global_device_ids=true | all-gather | bytes 655360 | tf_op jit(solution)/shard_map/all_gather | solution.py:83
  324.4 1.2 fusion.30
  325.6 0.0 all-reduce.5.cloned.1.call-start
  325.7 62.8 %all-reduce.3.cloned.1.call-done = f32[64,256]{1,0:T(8,128)} async-done(((f32[64,256]{1,0:T(8,128)}), f32[64,256]{1,0:T(8,128)}) %all-reduce.3.cloned.1.call-update) | async-done | bytes 65552 | tf_op jit(solution)/shard_map/psum | solution.py:89
  388.6 2.3 fusion.37
  390.9 103.7 %all-reduce.5.cloned.1.call-done = f32[64,256]{1,0:T(8,128)} async-done(((f32[64,256]{1,0:T(8,128)}), f32[64,256]{1,0:T(8,128)}) %all-reduce.5.cloned.1.call-update) | async-done | bytes 65552 | tf_op jit(solution)/shard_map/psum | solution.py:89
  494.6 26.3 %reduce-scatter.11.cloned.1.call-done = f32[64,512]{1,0:T(8,128)} async-done(((f32[256,512]{1,0:T(8,128)}), f32[64,512]{1,0:T(8,128)}) %reduce-scatter.11.cloned.1.call-update) | async-done | bytes 131088 | tf_op jit(solution)/shard_map/reduce_scatter | solution.py:70
  520.9 1.5 copy.33
  (30 shorter events, 0.3 us)
Async XLA Ops:
  7.2 1.0 copy-start
  7.2 33.5 %reduce-scatter.5.cloned.1.call-start = ((), (), s32[]{:S(2)}) async-start(), calls=%async_computation.4 | async-start | bytes 655360 | tf_op jit(solution)/shard_map/reduce_scatter | solution.py:46
  10.5 56.4 %all-gather.3.cloned.1.call-start = ((), (), s32[]{:S(2)}) async-start(), calls=%async_computation.5 | async-start | bytes 1179648 | tf_op jit(solution)/shard_map/all_gather | solution.py:58
  40.7 149.7 %reduce-scatter.7.cloned.1.call-start = ((), (), s32[]{:S(2)}) async-start(), calls=%async_computation.6 | async-start | bytes 1179648 | tf_op jit(solution)/shard_map/reduce_scatter | solution.py:62
  42.1 14.2 %copy-start.3 = (s32[160]{0:T(256)S(1)}, s32[160]{0:T(256)}, u32[]{:S(2)}) copy-start(s32[160]{0:T(256)} %param.17) | copy-start | bytes 1924
  42.1 14.2 %copy-start.5 = (s32[160]{0:T(256)S(1)}, s32[160]{0:T(256)}, u32[]{:S(2)}) copy-start(s32[160]{0:T(256)} %param.18) | copy-start | bytes 1924
  71.5 24.3 %copy-start.4 = (s32[160]{0:T(256)S(1)}, s32[160]{0:T(256)}, u32[]{:S(2)}) copy-start(s32[160]{0:T(256)} %param.16) | copy-start | bytes 1924
  95.8 94.6 %copy-start.2 = (f32[64,512]{1,0:T(8,128)S(1)}, f32[64,512]{1,0:T(8,128)}, u32[]{:S(2)}) copy-start(f32[64,512]{1,0:T(8,128)} %param.14) | copy-start | bytes 393220
  103.1 148.2 %all-gather.5.cloned.1.call-start = ((), (), s32[]{:S(2)}) async-start(), calls=%async_computation.7 | async-start | bytes 1179648 | tf_op jit(solution)/shard_map/all_gather | solution.py:65
  192.1 115.8 %reduce-scatter.9.cloned.1.call-start = ((), (), s32[]{:S(2)}) async-start(), calls=%async_computation.8 | async-start | bytes 1179648 | tf_op jit(solution)/shard_map/reduce_scatter | solution.py:69
  269.8 54.5 %copy-start.1 = (f32[64,512]{1,0:T(8,128)S(1)}, f32[64,512]{1,0:T(8,128)}, u32[]{:S(2)}) copy-start(f32[64,512]{1,0:T(8,128)} %param.12) | copy-start | bytes 393220
  277.1 111.4 %all-reduce.3.cloned.1.call-start = ((), (), s32[]{:S(2)}) async-start(), calls=%async_computation.10 | async-start | bytes 131072 | tf_op jit(solution)/shard_map/psum | solution.py:89
  325.6 169.0 %all-reduce.5.cloned.1.call-start = ((), (), s32[]{:S(2)}) async-start(), calls=%async_computation.11 | async-start | bytes 131072 | tf_op jit(solution)/shard_map/psum | solution.py:89
  388.5 132.4 %reduce-scatter.11.cloned.1.call-start = ((), (), s32[]{:S(2)}) async-start(), calls=%async_computation.9 | async-start | bytes 655360 | tf_op jit(solution)/shard_map/reduce_scatter | solution.py:70
Sparse Core Ops, SparseCore 0:
  10.6 30.0 reduce-scatter.4
  42.5 24.2 all-gather.2
  103.2 87.1 reduce-scatter.6
  193.4 57.8 all-gather.4
  277.2 30.6 reduce-scatter.8
  325.7 62.7 all-reduce.2
  391.1 103.4 all-reduce.4
  497.7 23.1 reduce-scatter.10
